TPU v7x, 256 devices: a whole 4x4x8 slice. The times are simulated.
256 devices in a mesh: seq: 64 (over x, z, core), head: 4 (over y).
Axes of the slice: x: 4, y: 4, z: 8, core: 2. Of those that a mesh axis runs over, the one named last changes fastest.
Arguments:
- q_latent: bfloat16 [16384, 1536], P('seq', 'head'), may hold values from -6 to 6
- kv_latent: bfloat16 [16384, 512], P('seq', 'head'), may hold values from -6 to 6
- k_rope: bfloat16 [16384, 64], P('seq'), may hold values from -6 to 6
- segment_ids: int32 [16384], P('seq'), may hold values from 0 to 63, as said below
- w_q_nope: bfloat16 [1536, 16384], P('seq', 'head'), may hold values from -6 to 6
- w_q_rope: bfloat16 [1536, 8192], P('seq', 'head'), may hold values from -6 to 6
- w_kv_nope: bfloat16 [512, 16384], P('seq', 'head'), may hold values from -6 to 6
- threshold: float32 [1], replicated, may hold values from 3.5 to 5.5
Outputs:
- new_q_nope: bfloat16 [1536, 16384], P('seq', 'head')
- new_q_rope: bfloat16 [1536, 8192], P('seq', 'head')
- new_kv_nope: bfloat16 [512, 16384], P('seq', 'head')
- head_max: float32 [128], P('head')
- row_max: float32 [16384, 128], P('seq', 'head')
Inputs may be any that keep to these rules, and one draw needn't show every extreme that they name: segment_ids never fall along the tokens and each document has 1 to 768 tokens.
All inputs are finite; a program needn't handle non-finite values.
Results may differ from a plain program's by a relative error of at most 0.0034.
Values may be sent and summed in bfloat16 or wider, within the bound.
No kernel may reach another device: no remote copies, remote signals or barrier semaphores. Data moves between devices by JAX's collectives and lax.ppermute only.
A program may use at most 128 MiB of HBM per device.

v0:
```python
import math
import jax
import jax.numpy as jnp
from jax import lax
from jax.sharding import PartitionSpec as P

D_NOPE = 128
D_ROPE = 64
QLORA = 1536
KVLORA = 512
REACH = 3


def joined_along(blocks, dim):
    blocks = jnp.moveaxis(blocks, 0, dim)
    lengths = blocks.shape
    return blocks.reshape(*lengths[:dim], lengths[dim] * lengths[dim + 1], *lengths[dim + 2 :])


def one_gather(arrays, axis, dims):
    ravelled = jnp.concatenate([a.reshape(-1) for a in arrays])
    lines, at, finished = (lax.all_gather(ravelled, axis), 0, [])
    for a, dim in zip(arrays, dims):
        blocks = lines[:, at : at + a.size].reshape(-1, *a.shape)
        finished.append(joined_along(blocks, dim))
        at += a.size
    return tuple(finished)


def side_by_side(arrays, axis, dim, along):
    both = jnp.concatenate(arrays, axis=along)
    result, at, finished = (lax.all_gather(both, axis, axis=dim, tiled=True), 0, [])
    for a in arrays:
        finished.append(lax.slice_in_dim(result, at, at + a.shape[along], axis=along))
        at += a.shape[along]
    return tuple(finished)


def shifted(block, axis, distance):
    devices = range(lax.axis_size(axis))
    route = [(i - distance, i) for i in devices if i - distance in devices]
    return lax.ppermute(block, axis, route)


def sent_to_all(value, axis):
    devices = lax.axis_size(axis)
    return lax.all_to_all(
        jnp.broadcast_to(value[None], (devices, *value.shape)), axis, 0, 0, tiled=True
    )


def over_copies(value, axis):
    everything = sent_to_all(value, axis)
    return jnp.max(everything, axis=0)


def score_max(query_nope, query_rope, key_nope, key_rope, allowed):
    nope = jnp.einsum("qhd,khd->hqk", query_nope, key_nope, preferred_element_type=jnp.float32)
    rope = jnp.einsum("qhd,kd->hqk", query_rope, key_rope, preferred_element_type=jnp.float32)
    scores = (nope + rope) * (1.0 / math.sqrt(D_NOPE + D_ROPE))
    return jnp.max(jnp.where(allowed[None], scores, jnp.float32(-1e30)), axis=2)


def masked_max(compute, operands):
    return compute(*operands)


def local(q_latent, kv_latent, k_rope, segment_ids, w_q_nope, w_q_rope, w_kv_nope, threshold):
    q_whole, kv_whole = one_gather((q_latent, kv_latent), "head", (1, 1))
    rows = q_whole.shape[0]
    heads = w_q_nope.shape[1] // D_NOPE
    q_scale = 1.0 / math.sqrt(QLORA)
    k_scale = 1.0 / math.sqrt(KVLORA)
    place = lax.axis_index("seq")
    full_nope, full_rope, full_kv = (
        *side_by_side((w_q_nope, w_q_rope), "seq", 0, 1),
        lax.all_gather(w_kv_nope, "seq", axis=0, tiled=True),
    )
    query_nope = (
        (jnp.dot(q_whole, full_nope, preferred_element_type=jnp.float32) * q_scale)
        .astype(jnp.bfloat16)
        .reshape(rows, heads, D_NOPE)
    )
    query_rope = (
        (jnp.dot(q_whole, full_rope, preferred_element_type=jnp.float32) * q_scale)
        .astype(jnp.bfloat16)
        .reshape(rows, heads, D_ROPE)
    )

    def expand(latent):
        return (
            (jnp.dot(latent, full_kv, preferred_element_type=jnp.float32) * k_scale)
            .astype(jnp.bfloat16)
            .reshape(rows, heads, D_NOPE)
        )

    def tokens_max(moving_first, moving_rope, allowed):
        key_nope = expand(moving_first)
        return score_max(query_nope, query_rope, key_nope, moving_rope, allowed)

    query_pos = place * rows + jnp.arange(rows, dtype=jnp.int32)
    moving = (kv_whole, k_rope)
    moving_seg = segment_ids
    running = jnp.full((heads, rows), -1e30, jnp.float32)
    for back in range(REACH + 1):
        if back > 0:
            moving = shifted((moving[0], moving[1]), "seq", 1)
            moving_seg = shifted(moving_seg, "seq", 1)
        key_pos = (place - back) * rows + jnp.arange(rows, dtype=jnp.int32)
        allowed = (
            (segment_ids[:, None] == moving_seg[None, :])
            & (key_pos[None, :] <= query_pos[:, None])
            & (key_pos[None, :] >= 0)
        )
        found = masked_max(tokens_max, (moving[0], moving[1], allowed))
        running = jnp.maximum(running, found)
    row_max = running.T
    local_heads = jnp.max(running, axis=1)
    head_max = over_copies(local_heads, "seq")
    clip = threshold[0] / jnp.maximum(head_max, threshold[0])
    root = jnp.sqrt(clip)
    new_q_nope = (w_q_nope.astype(jnp.float32) * jnp.repeat(root, D_NOPE)[None, :]).astype(
        jnp.bfloat16
    )
    new_q_rope = (w_q_rope.astype(jnp.float32) * jnp.repeat(clip, D_ROPE)[None, :]).astype(
        jnp.bfloat16
    )
    new_kv_nope = (w_kv_nope.astype(jnp.float32) * jnp.repeat(root, D_NOPE)[None, :]).astype(
        jnp.bfloat16
    )
    return (new_q_nope, new_q_rope, new_kv_nope, head_max, row_max)


def solution(mesh):
    in_specs = (
        P("seq", "head"),
        P("seq", "head"),
        P("seq", None),
        P("seq"),
        P("seq", "head"),
        P("seq", "head"),
        P("seq", "head"),
        P(),
    )
    out_specs = (P("seq", "head"), P("seq", "head"), P("seq", "head"), P("head"), P("seq", "head"))
    return jax.shard_map(local, mesh=mesh, in_specs=in_specs, out_specs=out_specs, check_vma=False)
```

profile of v0, /device:TPU:1, one launch (start us, length us, event | category | flops | bytes accessed | tf_op | source)
XLA Modules:
  0.0 283.7 jit_solution(593446844976654654)
XLA Ops:
  7.2 1.0 reshape.364
  8.3 1.6 pad_maximum_fusion.1
  9.9 0.7 all-gather.7.cloned.1.call-update
  10.6 1.7 pad_maximum_fusion
  12.4 4.9 %collective-permute-start = (s32[256]{0:T(256)}, s32[256]{0:T(256)S(1)}, u32[]{:S(2)}, u32[]{:S(2)}) collective-permute-start(s32[256]{0:T(256)} %param.11), channel_id=1, source_target_pairs={{0,4},{4,8},{8,12},{12,16},{16,20},{20,24},{24,28},{28,32},{32,36}... | collective-permute-start | bytes 3080 | tf_op jit(solution)/shard_map/ppermute | solution.py:42
  17.3 1.9 collective-permute-start.2
  19.3 20.2 %all-gather.9.cloned.1.call-done = bf16[524288]{0:T(1024)(128)(2,1)} async-done(((bf16[131072]{0:T(1024)(128)(2,1)}), bf16[524288]{0:T(1024)(128)(2,1)}) %all-gather.9.cloned.1.call-update) | async-done | bytes 1048592 | tf_op jit(solution)/shard_map/all_gather | solution.py:22
  39.4 1.6 reshape.376
  41.0 0.1 slice_bitcast_fusion
  41.2 0.1 copy.68
  41.3 4.6 %collective-permute-start.1 = (bf16[256,512]{0,1:T(8,128)(2,1)S(1)}, bf16[256,512]{0,1:T(8,128)(2,1)S(1)}, u32[]{:S(2)}, u32[]{:S(2)}) collective-permute-start(bf16[256,512]{0,1:T(8,128)(2,1)S(1)} %bitcast.115), channel_id=1, source_target_pairs={{0,4},{4,8},{8,12},{12,16},{16,20},{20,24},{24,28},{28,32},{32,36}... | collective-permute-start | bytes 786440 | tf_op jit(solution)/shard_map/ppermute | solution.py:42
  46.0 1.9 collective-permute-start.3
  48.0 1.3 collective-permute-done.3
  49.3 4.4 %collective-permute-start.6 = (s32[256]{0:T(256)S(1)}, s32[256]{0:T(256)S(1)}, u32[]{:S(2)}, u32[]{:S(2)}) collective-permute-start(s32[256]{0:T(256)S(1)} %collective-permute-done.3), channel_id=1, source_target_pairs={{0,4},{4,8},{8,12},{12,16},{16,20},{20,24},{24,28},{28,32},{32,36}... | collective-permute-start | bytes 3080 | tf_op jit(solution)/shard_map/ppermute | solution.py:42
  53.7 1.9 collective-permute-start.4
  55.7 3.6 %collective-permute-start.5 = (bf16[256,64]{0,1:T(8,128)(2,1)S(1)}, bf16[256,64]{0,1:T(8,128)(2,1)S(1)}, u32[]{:S(2)}, u32[]{:S(2)}) collective-permute-start(bf16[256,64]{0,1:T(8,128)(2,1)S(1)} %collective-permute-done.2), channel_id=1, source_target_pairs={{0,4},{4,8},{8,12},{12,16},{16,20},{20,24},{24,28},{28,32},{32,36}... | collective-permute-start | bytes 98312 | tf_op jit(solution)/shard_map/ppermute | solution.py:42
  59.3 0.6 and_and_fusion.3
  59.9 0.3 collective-permute-done.5
  60.3 4.2 %collective-permute-start.8 = (bf16[256,64]{0,1:T(8,128)(2,1)S(1)}, bf16[256,64]{0,1:T(8,128)(2,1)S(1)}, u32[]{:S(2)}, u32[]{:S(2)}) collective-permute-start(bf16[256,64]{0,1:T(8,128)(2,1)S(1)} %collective-permute-done.5), channel_id=1, source_target_pairs={{0,4},{4,8},{8,12},{12,16},{16,20},{20,24},{24,28},{28,32},{32,36}... | collective-permute-start | bytes 98312 | tf_op jit(solution)/shard_map/ppermute | solution.py:42
  64.5 0.3 slice.16
  64.8 0.1 copy.121
  64.9 0.3 copy.67
  65.2 1.9 collective-permute-start.7
  67.1 55.8 %all-gather.7.cloned.1.call-done = bf16[512,4096]{1,0:T(8,128)(2,1)} async-done(((bf16[8,4096]{1,0:T(8,128)(2,1)}), bf16[512,4096]{1,0:T(8,128)(2,1)}) %all-gather.7.cloned.1.call-update) | async-done | bytes 4194320 | tf_op jit(solution)/shard_map/all_gather | solution.py:77
  122.9 5.1 %fusion.52 = bf16[32,32,8,128]{3,2,1,0:T(8,128)(2,1)} fusion(bf16[256,512]{0,1:T(8,128)(2,1)S(1)} %collective-permute-done.4, bf16[512,4096]{1,0:T(8,128)(2,1)} %all-gather.7.cloned.1.call-done), kind=kOutput, calls=%fused_computation.50 | convolution fusion | flops 1075838976 | bytes 6553600 | tf_op jit(solution)/shard_map/dot_general | solution.py:92
  128.0 2.8 fusion.53
  130.8 2.8 fusion.54
  133.6 1.4 fusion.51
  135.0 92.9 %all-gather.5.cloned.1.call-done = bf16[1536,6144]{1,0:T(8,128)(2,1)} async-done(((bf16[24,6144]{1,0:T(8,128)(2,1)}), bf16[1536,6144]{1,0:T(8,128)(2,1)}) %all-gather.5.cloned.1.call-update) | async-done | bytes 18874384 | tf_op jit(solution)/shard_map/all_gather | solution.py:32
  227.9 5.7 %fusion.29 = bf16[256,2048]{1,0:T(8,128)(2,1)} fusion(bf16[256,1536]{0,1:T(8,128)(2,1)S(1)} %bitcast.122, bf16[1536,6144]{1,0:T(8,128)(2,1)} %all-gather.5.cloned.1.call-done), kind=kOutput, calls=%fused_computation.31 | convolution fusion | flops 1611661312 | bytes 8126464 | tf_op jit(solution)/shard_map/dot_general | solution.py:85
  233.6 1.7 copy.71
  235.2 8.6 %fusion.48 = bf16[32,32,8,128]{3,2,1,0:T(8,128)(2,1)S(1)} fusion(bf16[256,1536]{0,1:T(8,128)(2,1)} %bitcast.123, bf16[1536,6144]{1,0:T(8,128)(2,1)} %all-gather.5.cloned.1.call-done), kind=kOutput, calls=%fused_computation.48 | convolution fusion | flops 3223322624 | bytes 15466496 | tf_op jit(solution)/shard_map/dot_general | solution.py:80
  243.9 1.3 fusion.41
  245.2 0.3 copy-done.1
  245.5 1.3 fusion.38
  246.7 2.9 %fusion.35 = f32[32,256,256]{1,2,0:T(8,128)S(1)} fusion(bf16[32,32,8,128]{3,2,1,0:T(8,128)(2,1)} %fusion.52, bf16[32,32,8,128]{3,2,1,0:T(8,128)(2,1)S(1)} %fusion.48), kind=kOutput, calls=%fused_computation.35 | convolution fusion | flops 536870912 | bytes 12582912 | tf_op jit(solution)/shard_map/qhd,khd->hqk/dot_general | solution.py:58
  249.7 1.7 fusion.13
  251.4 1.7 fusion.10
  253.1 1.8 fusion.7
  254.9 1.6 fusion.32
  256.5 1.8 fusion.4
  258.3 0.7 fusion.64
  259.0 0.6 broadcast_in_dim.76
  259.7 6.0 %all-to-all-start = ((f32[64,1,32]{2,1,0:T(1,128)}), f32[64,1,32]{2,1,0:T(1,128)S(1)}, u32[]{:S(2)}, u32[]{:S(2)}) async-start(f32[64,1,32]{2,1,0:T(1,128)} %broadcast_in_dim.76), calls=%async_computation | async-start | bytes 65536 | tf_op jit(solution)/shard_map/all_to_all | solution.py:47
  266.3 8.6 %all-to-all-done = f32[64,1,32]{2,1,0:T(1,128)S(1)} async-done(((f32[64,1,32]{2,1,0:T(1,128)}), f32[64,1,32]{2,1,0:T(1,128)S(1)}, u32[]{:S(2)}, u32[]{:S(2)}) %all-to-all-start) | async-done | bytes 8224 | tf_op jit(solution)/shard_map/all_to_all | solution.py:47
  275.0 0.7 multiply_convert_fusion.2
  275.7 0.7 multiply_convert_fusion
  276.5 0.7 multiply_convert_fusion.1
  (41 shorter events, 0.6 us)
Async XLA Ops:
  7.2 52.1 %copy-start.7 = (s32[256]{0:T(256)S(1)}, s32[256]{0:T(256)}, u32[]{:S(2)}) copy-start(s32[256]{0:T(256)} %param.11) | copy-start | bytes 3076
  7.2 32.2 %all-gather.9.cloned.1.call-start = ((), (), s32[]{:S(2)}) async-start(), calls=%async_computation.3 | async-start | bytes 1310720 | tf_op jit(solution)/shard_map/all_gather | solution.py:22
  9.8 113.0 %all-gather.7.cloned.1.call-start = ((), (), s32[]{:S(2)}) async-start(), calls=%async_computation.2 | async-start | bytes 4259840 | tf_op jit(solution)/shard_map/all_gather | solution.py:77
  10.6 217.3 %all-gather.5.cloned.1.call-start = ((), (), s32[]{:S(2)}) async-start(), calls=%async_computation.1 | async-start | bytes 19169280 | tf_op jit(solution)/shard_map/all_gather | solution.py:32
  12.4 33.7 %collective-permute-start = (s32[256]{0:T(256)}, s32[256]{0:T(256)S(1)}, u32[]{:S(2)}, u32[]{:S(2)}) collective-permute-start(s32[256]{0:T(256)} %param.11), channel_id=1, source_target_pairs={{0,4},{4,8},{8,12},{12,16},{16,20},{20,24},{24,28},{28,32},{32,36}... | collective-permute-start | bytes 3080 | tf_op jit(solution)/shard_map/ppermute | solution.py:42
  17.3 38.4 %collective-permute-start.2 = (bf16[256,64]{0,1:T(8,128)(2,1)}, bf16[256,64]{0,1:T(8,128)(2,1)S(1)}, u32[]{:S(2)}, u32[]{:S(2)}) collective-permute-start(bf16[256,64]{0,1:T(8,128)(2,1)} %param.10), channel_id=1, source_target_pairs={{0,4},{4,8},{8,12},{12,16},{16,20},{20,24},{24,28},{28,32},{32,36}... | collective-permute-start | bytes 98312 | tf_op jit(solution)/shard_map/ppermute | solution.py:42
  41.3 12.4 %collective-permute-start.1 = (bf16[256,512]{0,1:T(8,128)(2,1)S(1)}, bf16[256,512]{0,1:T(8,128)(2,1)S(1)}, u32[]{:S(2)}, u32[]{:S(2)}) collective-permute-start(bf16[256,512]{0,1:T(8,128)(2,1)S(1)} %bitcast.115), channel_id=1, source_target_pairs={{0,4},{4,8},{8,12},{12,16},{16,20},{20,24},{24,28},{28,32},{32,36}... | collective-permute-start | bytes 786440 | tf_op jit(solution)/shard_map/ppermute | solution.py:42
  46.0 3.3 %collective-permute-start.3 = (s32[256]{0:T(256)S(1)}, s32[256]{0:T(256)S(1)}, u32[]{:S(2)}, u32[]{:S(2)}) collective-permute-start(s32[256]{0:T(256)S(1)} %collective-permute-done), channel_id=1, source_target_pairs={{0,4},{4,8},{8,12},{12,16},{16,20},{20,24},{24,28},{28,32},{32,36}... | collective-permute-start | bytes 3080 | tf_op jit(solution)/shard_map/ppermute | solution.py:42
  49.3 9.9 %collective-permute-start.6 = (s32[256]{0:T(256)S(1)}, s32[256]{0:T(256)S(1)}, u32[]{:S(2)}, u32[]{:S(2)}) collective-permute-start(s32[256]{0:T(256)S(1)} %collective-permute-done.3), channel_id=1, source_target_pairs={{0,4},{4,8},{8,12},{12,16},{16,20},{20,24},{24,28},{28,32},{32,36}... | collective-permute-start | bytes 3080 | tf_op jit(solution)/shard_map/ppermute | solution.py:42
  53.7 11.4 %collective-permute-start.4 = (bf16[256,512]{0,1:T(8,128)(2,1)S(1)}, bf16[256,512]{0,1:T(8,128)(2,1)S(1)}, u32[]{:S(2)}, u32[]{:S(2)}) collective-permute-start(bf16[256,512]{0,1:T(8,128)(2,1)S(1)} %collective-permute-done.1), channel_id=1, source_target_pairs={{0,4},{4,8},{8,12},{12,16},{16,20},{20,24},{24,28},{28,32},{32,36}... | collective-permute-start | bytes 786440 | tf_op jit(solution)/shard_map/ppermute | solution.py:42
  55.7 4.6 %collective-permute-start.5 = (bf16[256,64]{0,1:T(8,128)(2,1)S(1)}, bf16[256,64]{0,1:T(8,128)(2,1)S(1)}, u32[]{:S(2)}, u32[]{:S(2)}) collective-permute-start(bf16[256,64]{0,1:T(8,128)(2,1)S(1)} %collective-permute-done.2), channel_id=1, source_target_pairs={{0,4},{4,8},{8,12},{12,16},{16,20},{20,24},{24,28},{28,32},{32,36}... | collective-permute-start | bytes 98312 | tf_op jit(solution)/shard_map/ppermute | solution.py:42
  60.3 196.2 %collective-permute-start.8 = (bf16[256,64]{0,1:T(8,128)(2,1)S(1)}, bf16[256,64]{0,1:T(8,128)(2,1)S(1)}, u32[]{:S(2)}, u32[]{:S(2)}) collective-permute-start(bf16[256,64]{0,1:T(8,128)(2,1)S(1)} %collective-permute-done.5), channel_id=1, source_target_pairs={{0,4},{4,8},{8,12},{12,16},{16,20},{20,24},{24,28},{28,32},{32,36}... | collective-permute-start | bytes 98312 | tf_op jit(solution)/shard_map/ppermute | solution.py:42
  65.1 162.8 %copy-start.3 = (bf16[256,4,384]{0,2,1:T(8,128)(2,1)}, bf16[256,4,384]{0,2,1:T(8,128)(2,1)S(1)}, u32[]{:S(2)}) copy-start(bf16[256,4,384]{0,2,1:T(8,128)(2,1)S(1)} %copy.67) | copy-start | bytes 2359300
  65.2 68.4 %collective-permute-start.7 = (bf16[256,512]{0,1:T(8,128)(2,1)S(1)}, bf16[256,512]{0,1:T(8,128)(2,1)S(1)}, u32[]{:S(2)}, u32[]{:S(2)}) collective-permute-start(bf16[256,512]{0,1:T(8,128)(2,1)S(1)} %collective-permute-done.4), channel_id=1, source_target_pairs={{0,4},{4,8},{8,12},{12,16},{16,20},{20,24},{24,28},{28,32},{32,36}... | collective-permute-start | bytes 786440 | tf_op jit(solution)/shard_map/ppermute | solution.py:42
  122.9 5.1 %copy-start = (bf16[512,4096]{1,0:T(8,128)(2,1)S(1)}, bf16[512,4096]{1,0:T(8,128)(2,1)}, u32[]{:S(2)}) copy-start(bf16[512,4096]{1,0:T(8,128)(2,1)} %all-gather.7.cloned.1.call-done) | copy-start | bytes 12582916
  235.2 8.6 %copy-start.2 = (bf16[32,32,8,128]{3,2,1,0:T(8,128)(2,1)S(1)}, bf16[32,32,8,128]{3,2,1,0:T(8,128)(2,1)}, u32[]{:S(2)}) copy-start(bf16[32,32,8,128]{3,2,1,0:T(8,128)(2,1)} %fusion.54) | copy-start | bytes 6291460
  243.9 1.6 copy-start.1
  246.7 2.9 %copy-start.9 = (bf16[256,64]{0,1:T(8,128)(2,1)S(1)}, bf16[256,64]{0,1:T(8,128)(2,1)}, u32[]{:S(2)}) copy-start(bf16[256,64]{0,1:T(8,128)(2,1)} %param.10) | copy-start | bytes 98308
  256.5 18.5 %copy-start.6 = (bf16[8,4096]{1,0:T(8,128)(2,1)S(1)}, bf16[8,4096]{1,0:T(8,128)(2,1)}, u32[]{:S(2)}) copy-start(bf16[8,4096]{1,0:T(8,128)(2,1)} %param.14) | copy-start | bytes 196612
  256.5 19.2 %copy-start.4 = (bf16[24,4096]{1,0:T(8,128)(2,1)S(1)}, bf16[24,4096]{1,0:T(8,128)(2,1)}, u32[]{:S(2)}) copy-start(bf16[24,4096]{1,0:T(8,128)(2,1)} %param.12) | copy-start | bytes 589828
  256.5 20.0 %copy-start.5 = (bf16[24,2048]{1,0:T(8,128)(2,1)S(1)}, bf16[24,2048]{1,0:T(8,128)(2,1)}, u32[]{:S(2)}) copy-start(bf16[24,2048]{1,0:T(8,128)(2,1)} %param.13) | copy-start | bytes 294916
  259.7 15.2 %all-to-all-start = ((f32[64,1,32]{2,1,0:T(1,128)}), f32[64,1,32]{2,1,0:T(1,128)S(1)}, u32[]{:S(2)}, u32[]{:S(2)}) async-start(f32[64,1,32]{2,1,0:T(1,128)} %broadcast_in_dim.76), calls=%async_computation | async-start | bytes 65536 | tf_op jit(solution)/shard_map/all_to_all | solution.py:47
  274.9 2.3 copy-start.8
Sparse Core Ops, SparseCore 0:
  9.9 29.4 all-gather.8
  42.2 80.6 all-gather.6
  125.6 102.2 all-gather.4
where the time goes:
time: 284 us
  waiting for transfers between devices  180 us (63%)
  matrix products  40.4 us (14%)
  starting transfers between devices  35.5 us (12%)
  between operations  14.8 us (5%)
  other arithmetic  6.78 us (2%)
  local copies, waits for them, and re-layouts  6.44 us (2%)
    all_gather x1, waiting for transfers between devices, side_by_side(): lax.all_gather(both, axis, axis=dim, tiled=True)  92.9 us
    all_gather x1, waiting for transfers between devices, local(): lax.all_gather(w_kv_nope, 'seq', axis=0, tiled=True)  55.8 us
    ppermute x9, starting transfers between devices, shifted(): return lax.ppermute(block, axis, route)  29.4 us
    all_gather x1, waiting for transfers between devices, one_gather(): lines, at, finished = (lax.all_gather(ravelled, axis), 0, [])  20.2 us
    dot_general x4, matrix products, expand(): jnp.dot(latent, full_kv, preferred_element_type=jnp.float32) * k_scale  12.1 us
    dot_general x1, matrix products, local(): jnp.dot(q_whole, full_nope, preferred_element_type=jnp.float32) * q_scale  8.62 us
    all_to_all x1, waiting for transfers between devices, sent_to_all(): lax.all_to_all(jnp.broadcast_to(value[None], (devices, *value.shape)), ax...  8.56 us
    dot_general x4, matrix products, score_max(): jnp.einsum('qhd,khd->hqk', query_nope, key_nope, preferred_element_type=j...  7 us
  transfers between devices with their start and end apart: 13, of which 6 were waited for; matrix products, arithmetic and copies ran while one was open for 16% of the time, Pallas kernels for 0%

commit v1 on v0

--- a/solution.py
+++ b/solution.py
@@ -74,7 +74,9 @@
     place = lax.axis_index("seq")
     full_nope, full_rope, full_kv = (
         *side_by_side((w_q_nope, w_q_rope), "seq", 0, 1),
-        lax.all_gather(w_kv_nope, "seq", axis=0, tiled=True),
+        jnp.concatenate(
+            lax.all_to_all(jnp.stack([w_kv_nope] * lax.axis_size("seq")), "seq", 0, 0), axis=0
+        ),
     )
     query_nope = (
         (jnp.dot(q_whole, full_nope, preferred_element_type=jnp.float32) * q_scale)

time: 284 us -> 251 us (0.88)
  waiting for transfers between devices: 180 us -> 117 us
  starting transfers between devices: 35.5 us -> 55.1 us
  matrix products: 40.4 us -> 47 us
  local copies, waits for them, and re-layouts: 6.44 us -> 9.81 us
    ppermute x9, waiting for transfers between devices: 1.7 us -> 102 us  [shifted(): return lax.ppermute(block, axis, route)]
    all_gather x1, waiting for transfers between devices: 92.9 us -> 0.02 us  [side_by_side(): lax.all_gather(both, axis, axis=dim, tiled=True)]
    all_gather x1 -> x0, waiting for transfers between devices: 55.8 us -> none  [local(): lax.all_gather(w_kv_nope, 'seq', axis=0, tiled=True)]
    all_gather x1, waiting for transfers between devices: 20.2 us -> 5.48 us  [one_gather(): lines, at, finished = (lax.all_gather(ravelled, axis), 0, [])]
    all_to_all x0 -> x1, starting transfers between devices: none -> 13.3 us  [local(): lax.all_to_all(jnp.stack([w_kv_nope] * lax.axis_size('seq')), 'seq', 0, 0)]
    dot_general x4, matrix products: 12.1 us -> 18.9 us  [expand(): jnp.dot(latent, full_kv, preferred_element_type=jnp.float32) * k_scale]
    all_to_all x1, starting transfers between devices: 5.96 us -> 11.2 us  [sent_to_all(): lax.all_to_all(jnp.broadcast_to(value[None], (devices, *value.shape)), ax...]
    another operation x0 -> x1, local copies, waits for them, and re-layouts: none -> 3.38 us  [local(): jnp.stack([w_kv_nope] * lax.axis_size('seq'))]
  transfers between devices with their start and end apart: 13 -> 13, of which waited for: 6 -> 5; matrix products, arithmetic and copies ran while one was open for 16% -> 22% of each run, Pallas kernels for 0% -> 0%
where the time goes in v1:
time: 251 us; the launch traced here: 250 us
  waiting for transfers between devices  117 us (47%)
  starting transfers between devices  55.1 us (22%)
  matrix products  47 us (19%)
  between operations  15.1 us (6%)
  local copies, waits for them, and re-layouts  9.81 us (4%)
  other arithmetic  6.78 us (3%)
    ppermute x9, waiting for transfers between devices, shifted(): return lax.ppermute(block, axis, route)  102 us
    ppermute x9, starting transfers between devices, shifted(): return lax.ppermute(block, axis, route)  30.5 us
    dot_general x4, matrix products, expand(): jnp.dot(latent, full_kv, preferred_element_type=jnp.float32) * k_scale  18.9 us
    all_to_all x1, starting transfers between devices, local(): lax.all_to_all(jnp.stack([w_kv_nope] * lax.axis_size('seq')), 'seq', 0, 0)  13.3 us
    all_to_all x1, starting transfers between devices, sent_to_all(): lax.all_to_all(jnp.broadcast_to(value[None], (devices, *value.shape)), ax...  11.2 us
    dot_general x1, matrix products, local(): jnp.dot(q_whole, full_nope, preferred_element_type=jnp.float32) * q_scale  8.62 us
    all_to_all x1, waiting for transfers between devices, sent_to_all(): lax.all_to_all(jnp.broadcast_to(value[None], (devices, *value.shape)), ax...  8.56 us
    dot_general x4, matrix products, score_max(): jnp.einsum('qhd,khd->hqk', query_nope, key_nope, preferred_element_type=j...  6.97 us
  transfers between devices with their start and end apart: 13, of which 5 were waited for; matrix products, arithmetic and copies ran while one was open for 22% of the time, Pallas kernels for 0%

profile of v1, /device:TPU:1, one launch (start us, length us, event | category | flops | bytes accessed | tf_op | source)
XLA Modules:
  0.0 250.3 jit_solution(8710500390703430351)
XLA Ops:
  7.2 1.0 reshape.369
  8.2 1.6 pad_maximum_fusion.1
  9.9 1.7 pad_maximum_fusion
  11.6 3.4 %stack.2 = bf16[64,8,4096]{2,1,0:T(8,128)(2,1)} broadcast(bf16[8,4096]{1,0:T(8,128)(2,1)} %param.14), dimensions={1,2} | broadcast | bytes 4259840 | tf_op jit(solution)/shard_map/stack | solution.py:78
  15.0 13.3 %all-to-all-start = ((bf16[64,8,4096]{2,1,0:T(8,128)(2,1)}), bf16[64,8,4096]{2,1,0:T(8,128)(2,1)}, u32[]{:S(2)}, u32[]{:S(2)}) async-start(bf16[64,8,4096]{2,1,0:T(8,128)(2,1)} %stack.2), calls=%async_computation | async-start | bytes 8388608 | tf_op jit(solution)/shard_map/all_to_all | solution.py:78
  28.3 3.5 %collective-permute-start = (s32[256]{0:T(256)S(1)}, s32[256]{0:T(256)S(1)}, u32[]{:S(2)}, u32[]{:S(2)}) collective-permute-start(s32[256]{0:T(256)S(1)} %copy-done.6), channel_id=1, source_target_pairs={{0,4},{4,8},{8,12},{12,16},{16,20},{20,24},{24,28},{28,32},{32,36}... | collective-permute-start | bytes 3080 | tf_op jit(solution)/shard_map/ppermute | solution.py:42
  31.9 2.1 collective-permute-start.2
  33.9 5.5 %all-gather.6.cloned.1.call-done = bf16[524288]{0:T(1024)(128)(2,1)} async-done(((bf16[131072]{0:T(1024)(128)(2,1)}), bf16[524288]{0:T(1024)(128)(2,1)}) %all-gather.6.cloned.1.call-update) | async-done | bytes 1048592 | tf_op jit(solution)/shard_map/all_gather | solution.py:22
  39.4 1.6 reshape.382
  41.0 0.1 slice_bitcast_fusion
  41.2 0.1 copy.68
  41.3 4.6 %collective-permute-start.1 = (bf16[256,512]{0,1:T(8,128)(2,1)S(1)}, bf16[256,512]{0,1:T(8,128)(2,1)S(1)}, u32[]{:S(2)}, u32[]{:S(2)}) collective-permute-start(bf16[256,512]{0,1:T(8,128)(2,1)S(1)} %bitcast.128), channel_id=1, source_target_pairs={{0,4},{4,8},{8,12},{12,16},{16,20},{20,24},{24,28},{28,32},{32,36}... | collective-permute-start | bytes 786440 | tf_op jit(solution)/shard_map/ppermute | solution.py:42
  46.0 89.5 %collective-permute-done = s32[256]{0:T(256)S(1)} collective-permute-done((s32[256]{0:T(256)S(1)}, s32[256]{0:T(256)S(1)}, u32[]{:S(2)}, u32[]{:S(2)}) %collective-permute-start) | collective-permute-done | bytes 1056 | tf_op jit(solution)/shard_map/ppermute | solution.py:42
  135.5 5.0 %collective-permute-start.3 = (s32[256]{0:T(256)S(1)}, s32[256]{0:T(256)S(1)}, u32[]{:S(2)}, u32[]{:S(2)}) collective-permute-start(s32[256]{0:T(256)S(1)} %collective-permute-done), channel_id=1, source_target_pairs={{0,4},{4,8},{8,12},{12,16},{16,20},{20,24},{24,28},{28,32},{32,36}... | collective-permute-start | bytes 3080 | tf_op jit(solution)/shard_map/ppermute | solution.py:42
  140.5 6.3 %collective-permute-done.3 = s32[256]{0:T(256)S(1)} collective-permute-done((s32[256]{0:T(256)S(1)}, s32[256]{0:T(256)S(1)}, u32[]{:S(2)}, u32[]{:S(2)}) %collective-permute-start.3) | collective-permute-done | bytes 1056 | tf_op jit(solution)/shard_map/ppermute | solution.py:42
  146.8 4.4 %collective-permute-start.6 = (s32[256]{0:T(256)S(1)}, s32[256]{0:T(256)S(1)}, u32[]{:S(2)}, u32[]{:S(2)}) collective-permute-start(s32[256]{0:T(256)S(1)} %collective-permute-done.3), channel_id=1, source_target_pairs={{0,4},{4,8},{8,12},{12,16},{16,20},{20,24},{24,28},{28,32},{32,36}... | collective-permute-start | bytes 3080 | tf_op jit(solution)/shard_map/ppermute | solution.py:42
  151.2 1.9 collective-permute-start.4
  153.2 2.7 %collective-permute-start.5 = (bf16[256,64]{0,1:T(8,128)(2,1)S(1)}, bf16[256,64]{0,1:T(8,128)(2,1)S(1)}, u32[]{:S(2)}, u32[]{:S(2)}) collective-permute-start(bf16[256,64]{0,1:T(8,128)(2,1)S(1)} %collective-permute-done.2), channel_id=1, source_target_pairs={{0,4},{4,8},{8,12},{12,16},{16,20},{20,24},{24,28},{28,32},{32,36}... | collective-permute-start | bytes 98312 | tf_op jit(solution)/shard_map/ppermute | solution.py:42
  155.9 0.6 and_and_fusion.3
  156.5 6.6 %collective-permute-done.5 = bf16[256,64]{0,1:T(8,128)(2,1)S(1)} collective-permute-done((bf16[256,64]{0,1:T(8,128)(2,1)S(1)}, bf16[256,64]{0,1:T(8,128)(2,1)S(1)}, u32[]{:S(2)}, u32[]{:S(2)}) %collective-permute-start.5) | collective-permute-done | bytes 32800 | tf_op jit(solution)/shard_map/ppermute | solution.py:42
  163.1 4.4 %collective-permute-start.8 = (bf16[256,64]{0,1:T(8,128)(2,1)S(1)}, bf16[256,64]{0,1:T(8,128)(2,1)S(1)}, u32[]{:S(2)}, u32[]{:S(2)}) collective-permute-start(bf16[256,64]{0,1:T(8,128)(2,1)S(1)} %collective-permute-done.5), channel_id=1, source_target_pairs={{0,4},{4,8},{8,12},{12,16},{16,20},{20,24},{24,28},{28,32},{32,36}... | collective-permute-start | bytes 98312 | tf_op jit(solution)/shard_map/ppermute | solution.py:42
  167.5 0.3 slice.16
  167.8 0.1 copy.121
  167.9 0.3 copy.67
  168.2 1.9 collective-permute-start.7
  170.1 5.1 %fusion.61 = bf16[32,32,8,128]{3,2,1,0:T(8,128)(2,1)} fusion(bf16[256,512]{0,1:T(8,128)(2,1)S(1)} %collective-permute-done.1, bf16[64,8,4096]{2,1,0:T(8,128)(2,1)} %all-to-all-done), kind=kOutput, calls=%fused_computation.55 | convolution fusion | flops 1075838976 | bytes 6553600 | tf_op jit(solution)/shard_map/dot_general | solution.py:94
  175.2 5.0 %fusion.58 = bf16[32,32,8,128]{3,2,1,0:T(8,128)(2,1)} fusion(bf16[256,512]{0,1:T(8,128)(2,1)S(1)} %collective-permute-done.4, bf16[64,8,4096]{2,1,0:T(8,128)(2,1)} %all-to-all-done), kind=kOutput, calls=%fused_computation.54 | convolution fusion | flops 1075838976 | bytes 6553600 | tf_op jit(solution)/shard_map/dot_general | solution.py:94
  180.2 5.1 %fusion.64 = bf16[32,32,8,128]{3,2,1,0:T(8,128)(2,1)} fusion(bf16[256,512]{0,1:T(8,128)(2,1)S(1)} %bitcast.129, bf16[64,8,4096]{2,1,0:T(8,128)(2,1)} %all-to-all-done), kind=kOutput, calls=%fused_computation.56 | convolution fusion | flops 1075838976 | bytes 6553600 | tf_op jit(solution)/shard_map/dot_general | solution.py:94
  185.3 3.7 %fusion.55 = bf16[32,32,8,128]{3,2,1,0:T(8,128)(2,1)S(1)} fusion(bf16[256,512]{0,1:T(8,128)(2,1)S(1)} %collective-permute-done.7, bf16[64,8,4096]{2,1,0:T(8,128)(2,1)} %all-to-all-done), kind=kOutput, calls=%fused_computation.53 | convolution fusion | flops 1075838976 | bytes 6553600 | tf_op jit(solution)/shard_map/dot_general | solution.py:94
  189.1 5.6 %fusion.33 = bf16[256,2048]{1,0:T(8,128)(2,1)} fusion(bf16[256,1536]{0,1:T(8,128)(2,1)S(1)} %bitcast.135, bf16[1536,6144]{1,0:T(8,128)(2,1)} %all-gather.4.cloned.1.call-done), kind=kOutput, calls=%fused_computation.35 | convolution fusion | flops 1611661312 | bytes 8126464 | tf_op jit(solution)/shard_map/dot_general | solution.py:87
  194.6 1.7 copy.71
  196.3 8.6 %fusion.52 = bf16[32,32,8,128]{3,2,1,0:T(8,128)(2,1)S(1)} fusion(bf16[256,1536]{0,1:T(8,128)(2,1)} %bitcast.136, bf16[1536,6144]{1,0:T(8,128)(2,1)} %all-gather.4.cloned.1.call-done), kind=kOutput, calls=%fused_computation.52 | convolution fusion | flops 3223322624 | bytes 15466496 | tf_op jit(solution)/shard_map/dot_general | solution.py:82
  205.0 1.3 fusion.45
  206.2 0.3 copy-done
  206.5 1.3 fusion.39
  207.8 2.9 %fusion.42 = f32[32,256,256]{1,2,0:T(8,128)S(1)} fusion(bf16[32,32,8,128]{3,2,1,0:T(8,128)(2,1)} %fusion.61, bf16[32,32,8,128]{3,2,1,0:T(8,128)(2,1)S(1)} %fusion.52), kind=kOutput, calls=%fused_computation.42 | convolution fusion | flops 536870912 | bytes 12582912 | tf_op jit(solution)/shard_map/qhd,khd->hqk/dot_general | solution.py:58
  210.7 1.7 fusion.13
  212.4 1.7 fusion.7
  214.2 1.8 fusion.10
  215.9 1.6 fusion.36
  217.5 1.8 fusion.4
  219.3 0.7 fusion.76
  220.0 0.6 broadcast_in_dim.76
  220.7 11.2 %all-to-all-start.1 = ((f32[64,1,32]{2,1,0:T(1,128)}), f32[64,1,32]{2,1,0:T(1,128)S(1)}, u32[]{:S(2)}, u32[]{:S(2)}) async-start(f32[64,1,32]{2,1,0:T(1,128)} %broadcast_in_dim.76), calls=%async_computation.1 | async-start | bytes 65536 | tf_op jit(solution)/shard_map/all_to_all | solution.py:47
  232.6 8.6 %all-to-all-done.1 = f32[64,1,32]{2,1,0:T(1,128)S(1)} async-done(((f32[64,1,32]{2,1,0:T(1,128)}), f32[64,1,32]{2,1,0:T(1,128)S(1)}, u32[]{:S(2)}, u32[]{:S(2)}) %all-to-all-start.1) | async-done | bytes 8224 | tf_op jit(solution)/shard_map/all_to_all | solution.py:47
  241.3 0.7 multiply_convert_fusion.2
  242.0 0.7 multiply_convert_fusion
  242.8 0.7 multiply_convert_fusion.1
  (39 shorter events, 0.6 us)
Async XLA Ops:
  7.2 32.3 %all-gather.6.cloned.1.call-start = ((), (), s32[]{:S(2)}) async-start(), calls=%async_computation.3 | async-start | bytes 1310720 | tf_op jit(solution)/shard_map/all_gather | solution.py:22
  9.8 179.2 %all-gather.4.cloned.1.call-start = ((), (), s32[]{:S(2)}) async-start(), calls=%async_computation.2 | async-start | bytes 19169280 | tf_op jit(solution)/shard_map/all_gather | solution.py:32
  15.0 13.3 %copy-start.6 = (s32[256]{0:T(256)S(1)}, s32[256]{0:T(256)}, u32[]{:S(2)}) copy-start(s32[256]{0:T(256)} %param.11) | copy-start | bytes 3076
  15.0 16.9 %copy-start.8 = (bf16[256,64]{0,1:T(8,128)(2,1)S(1)}, bf16[256,64]{0,1:T(8,128)(2,1)}, u32[]{:S(2)}) copy-start(bf16[256,64]{0,1:T(8,128)(2,1)} %param.10) | copy-start | bytes 98308
  15.0 155.1 %all-to-all-start = ((bf16[64,8,4096]{2,1,0:T(8,128)(2,1)}), bf16[64,8,4096]{2,1,0:T(8,128)(2,1)}, u32[]{:S(2)}, u32[]{:S(2)}) async-start(bf16[64,8,4096]{2,1,0:T(8,128)(2,1)} %stack.2), calls=%async_computation | async-start | bytes 8388608 | tf_op jit(solution)/shard_map/all_to_all | solution.py:78
  28.3 107.2 %collective-permute-start = (s32[256]{0:T(256)S(1)}, s32[256]{0:T(256)S(1)}, u32[]{:S(2)}, u32[]{:S(2)}) collective-permute-start(s32[256]{0:T(256)S(1)} %copy-done.6), channel_id=1, source_target_pairs={{0,4},{4,8},{8,12},{12,16},{16,20},{20,24},{24,28},{28,32},{32,36}... | collective-permute-start | bytes 3080 | tf_op jit(solution)/shard_map/ppermute | solution.py:42
  31.9 121.3 %collective-permute-start.2 = (bf16[256,64]{0,1:T(8,128)(2,1)S(1)}, bf16[256,64]{0,1:T(8,128)(2,1)S(1)}, u32[]{:S(2)}, u32[]{:S(2)}) collective-permute-start(bf16[256,64]{0,1:T(8,128)(2,1)S(1)} %copy-done.8), channel_id=1, source_target_pairs={{0,4},{4,8},{8,12},{12,16},{16,20},{20,24},{24,28},{28,32},{32,36}... | collective-permute-start | bytes 98312 | tf_op jit(solution)/shard_map/ppermute | solution.py:42
  41.3 109.9 %collective-permute-start.1 = (bf16[256,512]{0,1:T(8,128)(2,1)S(1)}, bf16[256,512]{0,1:T(8,128)(2,1)S(1)}, u32[]{:S(2)}, u32[]{:S(2)}) collective-permute-start(bf16[256,512]{0,1:T(8,128)(2,1)S(1)} %bitcast.128), channel_id=1, source_target_pairs={{0,4},{4,8},{8,12},{12,16},{16,20},{20,24},{24,28},{28,32},{32,36}... | collective-permute-start | bytes 786440 | tf_op jit(solution)/shard_map/ppermute | solution.py:42
  135.5 11.3 %collective-permute-start.3 = (s32[256]{0:T(256)S(1)}, s32[256]{0:T(256)S(1)}, u32[]{:S(2)}, u32[]{:S(2)}) collective-permute-start(s32[256]{0:T(256)S(1)} %collective-permute-done), channel_id=1, source_target_pairs={{0,4},{4,8},{8,12},{12,16},{16,20},{20,24},{24,28},{28,32},{32,36}... | collective-permute-start | bytes 3080 | tf_op jit(solution)/shard_map/ppermute | solution.py:42
  146.8 9.0 %collective-permute-start.6 = (s32[256]{0:T(256)S(1)}, s32[256]{0:T(256)S(1)}, u32[]{:S(2)}, u32[]{:S(2)}) collective-permute-start(s32[256]{0:T(256)S(1)} %collective-permute-done.3), channel_id=1, source_target_pairs={{0,4},{4,8},{8,12},{12,16},{16,20},{20,24},{24,28},{28,32},{32,36}... | collective-permute-start | bytes 3080 | tf_op jit(solution)/shard_map/ppermute | solution.py:42
  151.2 16.9 %collective-permute-start.4 = (bf16[256,512]{0,1:T(8,128)(2,1)S(1)}, bf16[256,512]{0,1:T(8,128)(2,1)S(1)}, u32[]{:S(2)}, u32[]{:S(2)}) collective-permute-start(bf16[256,512]{0,1:T(8,128)(2,1)S(1)} %collective-permute-done.1), channel_id=1, source_target_pairs={{0,4},{4,8},{8,12},{12,16},{16,20},{20,24},{24,28},{28,32},{32,36}... | collective-permute-start | bytes 786440 | tf_op jit(solution)/shard_map/ppermute | solution.py:42
  153.2 9.9 %collective-permute-start.5 = (bf16[256,64]{0,1:T(8,128)(2,1)S(1)}, bf16[256,64]{0,1:T(8,128)(2,1)S(1)}, u32[]{:S(2)}, u32[]{:S(2)}) collective-permute-start(bf16[256,64]{0,1:T(8,128)(2,1)S(1)} %collective-permute-done.2), channel_id=1, source_target_pairs={{0,4},{4,8},{8,12},{12,16},{16,20},{20,24},{24,28},{28,32},{32,36}... | collective-permute-start | bytes 98312 | tf_op jit(solution)/shard_map/ppermute | solution.py:42
  163.1 54.4 %collective-permute-start.8 = (bf16[256,64]{0,1:T(8,128)(2,1)S(1)}, bf16[256,64]{0,1:T(8,128)(2,1)S(1)}, u32[]{:S(2)}, u32[]{:S(2)}) collective-permute-start(bf16[256,64]{0,1:T(8,128)(2,1)S(1)} %collective-permute-done.5), channel_id=1, source_target_pairs={{0,4},{4,8},{8,12},{12,16},{16,20},{20,24},{24,28},{28,32},{32,36}... | collective-permute-start | bytes 98312 | tf_op jit(solution)/shard_map/ppermute | solution.py:42
  168.2 20.9 %copy-start.2 = (bf16[256,4,384]{0,2,1:T(8,128)(2,1)}, bf16[256,4,384]{0,2,1:T(8,128)(2,1)S(1)}, u32[]{:S(2)}) copy-start(bf16[256,4,384]{0,2,1:T(8,128)(2,1)S(1)} %copy.67) | copy-start | bytes 2359300
  168.2 17.1 %collective-permute-start.7 = (bf16[256,512]{0,1:T(8,128)(2,1)S(1)}, bf16[256,512]{0,1:T(8,128)(2,1)S(1)}, u32[]{:S(2)}, u32[]{:S(2)}) collective-permute-start(bf16[256,512]{0,1:T(8,128)(2,1)S(1)} %collective-permute-done.4), channel_id=1, source_target_pairs={{0,4},{4,8},{8,12},{12,16},{16,20},{20,24},{24,28},{28,32},{32,36}... | collective-permute-start | bytes 786440 | tf_op jit(solution)/shard_map/ppermute | solution.py:42
  196.3 8.6 %copy-start.1 = (bf16[32,32,8,128]{3,2,1,0:T(8,128)(2,1)S(1)}, bf16[32,32,8,128]{3,2,1,0:T(8,128)(2,1)}, u32[]{:S(2)}) copy-start(bf16[32,32,8,128]{3,2,1,0:T(8,128)(2,1)} %fusion.64) | copy-start | bytes 6291460
  205.0 1.6 copy-start
  217.5 23.8 %copy-start.5 = (bf16[8,4096]{1,0:T(8,128)(2,1)S(1)}, bf16[8,4096]{1,0:T(8,128)(2,1)}, u32[]{:S(2)}) copy-start(bf16[8,4096]{1,0:T(8,128)(2,1)} %param.14) | copy-start | bytes 196612
  217.5 24.5 %copy-start.3 = (bf16[24,4096]{1,0:T(8,128)(2,1)S(1)}, bf16[24,4096]{1,0:T(8,128)(2,1)}, u32[]{:S(2)}) copy-start(bf16[24,4096]{1,0:T(8,128)(2,1)} %param.12) | copy-start | bytes 589828
  217.5 25.3 %copy-start.4 = (bf16[24,2048]{1,0:T(8,128)(2,1)S(1)}, bf16[24,2048]{1,0:T(8,128)(2,1)}, u32[]{:S(2)}) copy-start(bf16[24,2048]{1,0:T(8,128)(2,1)} %param.13) | copy-start | bytes 294916
  220.7 20.5 %all-to-all-start.1 = ((f32[64,1,32]{2,1,0:T(1,128)}), f32[64,1,32]{2,1,0:T(1,128)S(1)}, u32[]{:S(2)}, u32[]{:S(2)}) async-start(f32[64,1,32]{2,1,0:T(1,128)} %broadcast_in_dim.76), calls=%async_computation.1 | async-start | bytes 65536 | tf_op jit(solution)/shard_map/all_to_all | solution.py:47
  241.2 2.3 copy-start.7
Sparse Core Ops, SparseCore 0:
  9.9 29.4 all-gather.5
  42.2 146.6 all-gather.3
